TPU v7x, 32 devices: a whole 2x2x4 slice. The times are simulated.
32 devices in a mesh: groups: 2 (over x), slab: 16 (over z, y, core).
Axes of the slice: x: 2, y: 2, z: 4, core: 2. Of those that a mesh axis runs over, the one named last changes fastest.
Arguments:
- activations: bfloat16 [2048, 65536], P(('groups', 'slab')), parts along dimension 0, may hold values from 0 to 4
- weights: bfloat16 [6, 2, 512, 128, 128], P(None, None, 'slab'), may hold values from -0.5 to 0.5
- biases: float32 [6, 65536], P(None, 'slab'), may hold values from -1 to 0.5
- columns: int32 [6, 512], P(None, 'slab'), may hold values from 0 to 31
Outputs:
- features: bfloat16 [2048, 65536], P(('groups', 'slab')), parts along dimension 0
There are 2 independent parts, one for each index of `groups`. A program takes and returns all parts, laid end to end along the dimension named above; an argument that names none is the same for every part. Nothing has to cross between parts.
Inputs may be any that keep to these rules, and one draw needn't show every extreme that they name: columns name a block within a group of 32 consecutive blocks.
All inputs are finite; a program needn't handle non-finite values.
Results may differ from a plain program's by a relative error of at most 0.0072.
Values may be sent and summed in bfloat16 or wider, within the bound.
No kernel may reach another device: no remote copies, remote signals or barrier semaphores. Data moves between devices by JAX's collectives and lax.ppermute only.
A program may use at most 128 MiB of HBM per device.

v0:
```python
import jax
import jax.numpy as jnp
from jax import lax
from jax.sharding import PartitionSpec as P

ceiling = 4.0


def from_partner(block, axis, bit):
    count = lax.axis_size(axis)
    route = []
    for low in range(count):
        high = low | 1 << bit
        if high != low and high < count:
            route += [(low, high), (high, low)]
    return lax.ppermute(block, axis, route)


def section_bit(section, remote, log_count):
    return (remote - 1 - section) * (log_count - 1) // (remote - 1)


def local(activations, weights, biases, columns):
    slab_count = lax.axis_size("slab")
    log_count = slab_count.bit_length() - 1
    layer_count = weights.shape[0]
    per_device = weights.shape[2]
    block_width = weights.shape[3]
    local_rows = activations.shape[0]
    remote = (layer_count + 1) // 2
    grouped = activations.reshape(local_rows, slab_count, per_device * block_width)
    stride = 1 << section_bit(0, remote, log_count)
    flipped = grouped.reshape(
        local_rows, slab_count // (2 * stride), 2, stride, per_device * block_width
    )
    flipped = flipped[:, :, ::-1].reshape(local_rows, slab_count, per_device * block_width)
    paired = jnp.stack([grouped, flipped], axis=2)
    arrived = lax.all_to_all(paired, "slab", split_axis=1, concat_axis=0, tiled=True)
    current = arrived[:, 0, 0].reshape(-1, per_device, block_width)
    first_cross = arrived[:, 0, 1].reshape(-1, per_device, block_width)
    for layer_index in range(layer_count):
        if layer_index % 2 == 0:
            if layer_index == 0 and first_cross is not None:
                source = first_cross
            else:
                source = from_partner(
                    current, "slab", section_bit(layer_index // 2, remote, log_count)
                )
        else:
            source = current
        crossing = jnp.take(source, columns[layer_index], axis=1)
        summed = jnp.einsum(
            "rkb,kbc->rkc", current, weights[layer_index, 0], preferred_element_type=jnp.float32
        )
        summed = summed + jnp.einsum(
            "rkb,kbc->rkc", crossing, weights[layer_index, 1], preferred_element_type=jnp.float32
        )
        summed = summed + biases[layer_index].reshape(per_device, block_width)
        current = jnp.clip(summed, 0.0, ceiling).astype(jnp.bfloat16)
    flattened = current.reshape(current.shape[0], per_device * block_width)
    return lax.all_to_all(flattened, "slab", split_axis=0, concat_axis=1, tiled=True)


def solution(mesh):
    placed = (
        P(("groups", "slab"), None),
        P(None, None, "slab", None, None),
        P(None, "slab"),
        P(None, "slab"),
    )
    return jax.shard_map(
        local, mesh=mesh, in_specs=placed, out_specs=P(("groups", "slab"), None), check_vma=False
    )
```

profile of v0, /device:TPU:1, one launch (start us, length us, event | category | flops | bytes accessed | tf_op | source)
XLA Modules:
  0.0 1066.5 jit_solution(5412748452448401006)
XLA Ops:
  0.0 12.1 %copy.28 = bf16[8,8,16,4096]{3,2,1,0:T(8,128)(2,1)} copy(bf16[8,8,16,4096]{3,1,2,0:T(8,128)(2,1)} %bitcast.134) | data formatting | bytes 16777216
  27.9 21.4 %copy.18 = bf16[64,16,2,4096]{3,0,2,1:T(8,128)(2,1)} copy(bf16[64,16,2,4096]{3,1,0,2:T(8,128)(2,1)S(1)} %pad_maximum_fusion) | data formatting | bytes 33554432 | tf_op jit(solution)/shard_map/stack | solution.py:37
  58.6 295.9 %all-to-all-done = bf16[64,16,2,4096]{3,0,2,1:T(8,128)(2,1)} async-done(((bf16[64,16,2,4096]{3,0,2,1:T(8,128)(2,1)}), bf16[64,16,2,4096]{3,0,2,1:T(8,128)(2,1)}, u32[]{:S(2)}, u32[]{:S(2)}) %all-to-all-start) | async-done | bytes 16777248 | tf_op jit(solution)/shard_map/all_to_all | solution.py:38
  369.2 12.0 %copy.22 = bf16[1024,1,1,4096]{0,3,2,1:T(8,128)(2,1)} copy(bf16[1024,1,1,4096]{3,0,2,1:T(8,128)(2,1)} %get-tuple-element.18) | data formatting | bytes 16777216 | tf_op jit(solution)/shard_map/slice | solution.py:40
  381.1 11.4 %copy.23 = bf16[1024,32,128]{2,0,1:T(8,128)(2,1)} copy(bf16[1024,32,128]{0,2,1:T(8,128)(2,1)} %bitcast.132) | data formatting | bytes 16777216 | tf_op jit(solution)/shard_map/reshape;squeeze | solution.py:40
  392.5 11.9 %copy.20 = bf16[1024,1,1,4096]{0,3,2,1:T(8,128)(2,1)} copy(bf16[1024,1,1,4096]{3,0,2,1:T(8,128)(2,1)} %get-tuple-element.19) | data formatting | bytes 16777216 | tf_op jit(solution)/shard_map/slice | solution.py:39
  412.8 11.8 %fusion.58 = f32[32,1024,128]{2,1,0:T(8,128)} fusion(bf16[1024,32,128]{0,2,1:T(8,128)(2,1)} %bitcast.131, bf16[6,2,32,128,128]{4,3,2,1,0:T(8,128)(2,1)} %param.7), kind=kOutput, calls=%fused_computation.60 | convolution fusion | flops 1073741824 | bytes 26214400 | tf_op jit(solution)/shard_map/rkb,kbc->rkc/dot_general | solution.py:52
  424.6 13.5 %fusion.18 = bf16[1024,32,128]{2,0,1:T(8,128)(2,1)} fusion(f32[32,128]{1,0:T(8,128)S(1)} %bitcast.140, f32[32,1024,128]{2,1,0:T(8,128)} %fusion.58, bf16[32,1024,128]{2,1,0:T(8,128)(2,1)} %gather_fusion, pred[32]{0:T(512)(128)(4,1)S(1)} %get-tuple-element.32, bf16[6,2,32,128,128]{4,3,2,1,0:T(8,128)(2,1)} %param.7), kind=kOutput, calls=%fused_computation.32 | convolution fusion | flops 1094713344 | bytes 34619424 | tf_op jit(solution)/shard_map/rkb,kbc->rkc/dot_general | solution.py:55
  438.2 11.7 %fusion.55 = f32[32,1024,128]{2,1,0:T(8,128)} fusion(bf16[1024,32,128]{2,0,1:T(8,128)(2,1)} %fusion.18, bf16[6,2,32,128,128]{4,3,2,1,0:T(8,128)(2,1)} %param.7), kind=kOutput, calls=%fused_computation.57 | convolution fusion | flops 1073741824 | bytes 26214400 | tf_op jit(solution)/shard_map/rkb,kbc->rkc/dot_general | solution.py:52
  458.2 13.7 %fusion.21 = bf16[1024,32,128]{2,0,1:T(8,128)(2,1)} fusion(f32[32,128]{1,0:T(8,128)S(1)} %bitcast.139, f32[32,1024,128]{2,1,0:T(8,128)} %fusion.55, bf16[32,1024,128]{2,1,0:T(8,128)(2,1)} %gather_fusion.1, pred[32]{0:T(512)(128)(4,1)S(1)} %get-tuple-element.30, bf16[6,2,32,128,128]{4,3,2,1,0:T(8,128)(2,1)} %param.7), kind=kOutput, calls=%fused_computation.33 | convolution fusion | flops 1094713344 | bytes 34619424 | tf_op jit(solution)/shard_map/rkb,kbc->rkc/dot_general | solution.py:55
  471.9 22.8 %collective-permute-start = (bf16[1024,32,128]{2,0,1:T(8,128)(2,1)}, bf16[1024,32,128]{2,0,1:T(8,128)(2,1)}, u32[]{:S(2)}, u32[]{:S(2)}) collective-permute-start(bf16[1024,32,128]{2,0,1:T(8,128)(2,1)} %fusion.21), channel_id=1, source_target_pairs={{0,2},{2,0},{1,3},{3,1},{4,6},{6,4},{5,7},{7,5},{8,10},{10,8},{9,1... | collective-permute-start | bytes 25165832 | tf_op jit(solution)/shard_map/ppermute | solution.py:16
  494.7 11.7 %fusion.52 = f32[32,1024,128]{2,1,0:T(8,128)} fusion(bf16[1024,32,128]{2,0,1:T(8,128)(2,1)} %fusion.21, bf16[6,2,32,128,128]{4,3,2,1,0:T(8,128)(2,1)} %param.7), kind=kOutput, calls=%fused_computation.54 | convolution fusion | flops 1073741824 | bytes 26214400 | tf_op jit(solution)/shard_map/rkb,kbc->rkc/dot_general | solution.py:52
  506.4 169.1 %collective-permute-done = bf16[1024,32,128]{2,0,1:T(8,128)(2,1)} collective-permute-done((bf16[1024,32,128]{2,0,1:T(8,128)(2,1)}, bf16[1024,32,128]{2,0,1:T(8,128)(2,1)}, u32[]{:S(2)}, u32[]{:S(2)}) %collective-permute-start) | collective-permute-done | bytes 8388640 | tf_op jit(solution)/shard_map/ppermute | solution.py:16
  684.1 13.5 %fusion.24 = bf16[1024,32,128]{2,0,1:T(8,128)(2,1)} fusion(f32[32,128]{1,0:T(8,128)S(1)} %bitcast.138, f32[32,1024,128]{2,1,0:T(8,128)} %fusion.52, bf16[32,1024,128]{2,1,0:T(8,128)(2,1)} %gather_fusion.2, pred[32]{0:T(512)(128)(4,1)S(1)} %get-tuple-element.28, bf16[6,2,32,128,128]{4,3,2,1,0:T(8,128)(2,1)} %param.7), kind=kOutput, calls=%fused_computation.34 | convolution fusion | flops 1094713344 | bytes 34619424 | tf_op jit(solution)/shard_map/rkb,kbc->rkc/dot_general | solution.py:55
  697.6 11.7 %fusion.49 = f32[32,1024,128]{2,1,0:T(8,128)} fusion(bf16[1024,32,128]{2,0,1:T(8,128)(2,1)} %fusion.24, bf16[6,2,32,128,128]{4,3,2,1,0:T(8,128)(2,1)} %param.7), kind=kOutput, calls=%fused_computation.51 | convolution fusion | flops 1073741824 | bytes 26214400 | tf_op jit(solution)/shard_map/rkb,kbc->rkc/dot_general | solution.py:52
  717.8 13.5 %fusion.27 = bf16[1024,32,128]{2,0,1:T(8,128)(2,1)} fusion(f32[32,128]{1,0:T(8,128)S(1)} %bitcast.137, f32[32,1024,128]{2,1,0:T(8,128)} %fusion.49, bf16[32,1024,128]{2,1,0:T(8,128)(2,1)} %gather_fusion.3, pred[32]{0:T(512)(128)(4,1)S(1)} %get-tuple-element.26, bf16[6,2,32,128,128]{4,3,2,1,0:T(8,128)(2,1)} %param.7), kind=kOutput, calls=%fused_computation.35 | convolution fusion | flops 1094713344 | bytes 34619424 | tf_op jit(solution)/shard_map/rkb,kbc->rkc/dot_general | solution.py:55
  731.7 11.7 %fusion.46 = f32[32,1024,128]{2,1,0:T(8,128)} fusion(bf16[1024,32,128]{2,0,1:T(8,128)(2,1)} %fusion.27, bf16[6,2,32,128,128]{4,3,2,1,0:T(8,128)(2,1)} %param.7), kind=kOutput, calls=%fused_computation.48 | convolution fusion | flops 1073741824 | bytes 26214400 | tf_op jit(solution)/shard_map/rkb,kbc->rkc/dot_general | solution.py:52
  744.8 8.8 gather_fusion.4
  753.6 13.5 %fusion.30 = bf16[1024,32,128]{2,0,1:T(8,128)(2,1)} fusion(f32[32,128]{1,0:T(8,128)S(1)} %bitcast.136, f32[32,1024,128]{2,1,0:T(8,128)} %fusion.46, bf16[32,1024,128]{2,1,0:T(8,128)(2,1)} %gather_fusion.4, pred[32]{0:T(512)(128)(4,1)S(1)} %get-tuple-element.34, bf16[6,2,32,128,128]{4,3,2,1,0:T(8,128)(2,1)} %param.7), kind=kOutput, calls=%fused_computation.36 | convolution fusion | flops 1094713344 | bytes 34619424 | tf_op jit(solution)/shard_map/rkb,kbc->rkc/dot_general | solution.py:55
  767.1 11.7 %fusion.43 = f32[32,1024,128]{2,1,0:T(8,128)} fusion(bf16[1024,32,128]{2,0,1:T(8,128)(2,1)} %fusion.30, bf16[6,2,32,128,128]{4,3,2,1,0:T(8,128)(2,1)} %param.7), kind=kOutput, calls=%fused_computation.45 | convolution fusion | flops 1073741824 | bytes 26214400 | tf_op jit(solution)/shard_map/rkb,kbc->rkc/dot_general | solution.py:52
  787.4 13.7 %fusion.33 = bf16[1024,32,128]{2,0,1:T(8,128)(2,1)} fusion(f32[32,128]{1,0:T(8,128)S(1)} %bitcast.135, f32[32,1024,128]{2,1,0:T(8,128)} %fusion.43, bf16[32,1024,128]{2,1,0:T(8,128)(2,1)} %gather_fusion.5, pred[32]{0:T(512)(128)(4,1)S(1)} %copy-done.3, bf16[6,2,32,128,128]{4,3,2,1,0:T(8,128)(2,1)} %param.7), kind=kOutput, calls=%fused_computation.37 | convolution fusion | flops 1094713344 | bytes 34619424 | tf_op jit(solution)/shard_map/rkb,kbc->rkc/dot_general | solution.py:55
  801.1 12.2 %copy.24 = bf16[1024,32,128]{2,1,0:T(8,128)(2,1)} copy(bf16[1024,32,128]{2,0,1:T(8,128)(2,1)} %fusion.33) | data formatting | bytes 16777216 | tf_op jit(solution)/shard_map/convert_element_type | solution.py:59
  813.3 13.3 %all_to_all.31 = bf16[16,64,4096]{2,1,0:T(8,128)(2,1)} reshape(bf16[1024,32,128]{2,1,0:T(8,128)(2,1)} %copy.24) | data formatting | bytes 16777216 | tf_op jit(solution)/shard_map/all_to_all | solution.py:61
  826.6 231.7 %all_to_all.37 = bf16[16,64,4096]{2,1,0:T(8,128)(2,1)} all-to-all(bf16[16,64,4096]{2,1,0:T(8,128)(2,1)} %all_to_all.31), channel_id=1, replica_groups=mesh['groups'=2,'slab'=16] {'slab'}, dimensions={0} | all-to-all | bytes 16777216 | tf_op jit(solution)/shard_map/all_to_all | solution.py:61
  (26 shorter events, 92.0 us)
Async XLA Ops:
  49.2 8.2 copy-start.2
  49.2 8.7 copy-start
  49.2 305.2 %all-to-all-start = ((bf16[64,16,2,4096]{3,0,2,1:T(8,128)(2,1)}), bf16[64,16,2,4096]{3,0,2,1:T(8,128)(2,1)}, u32[]{:S(2)}, u32[]{:S(2)}) async-start(bf16[64,16,2,4096]{3,0,2,1:T(8,128)(2,1)} %copy.18), calls=%async_computation | async-start | bytes 33554432 | tf_op jit(solution)/shard_map/all_to_all | solution.py:38
  471.9 203.6 %collective-permute-start = (bf16[1024,32,128]{2,0,1:T(8,128)(2,1)}, bf16[1024,32,128]{2,0,1:T(8,128)(2,1)}, u32[]{:S(2)}, u32[]{:S(2)}) collective-permute-start(bf16[1024,32,128]{2,0,1:T(8,128)(2,1)} %fusion.21), channel_id=1, source_target_pairs={{0,2},{2,0},{1,3},{3,1},{4,6},{6,4},{5,7},{7,5},{8,10},{10,8},{9,1... | collective-permute-start | bytes 25165832 | tf_op jit(solution)/shard_map/ppermute | solution.py:16
  731.3 13.5 %collective-permute-start.1 = (bf16[1024,32,128]{2,0,1:T(8,128)(2,1)}, bf16[1024,32,128]{2,0,1:T(8,128)(2,1)}, u32[]{:S(2)}, u32[]{:S(2)}) collective-permute-start(bf16[1024,32,128]{2,0,1:T(8,128)(2,1)} %fusion.27), channel_id=1, source_target_pairs={{0,1},{1,0},{2,3},{3,2},{4,5},{5,4},{6,7},{7,6},{8,9},{9,8},{10,11... | collective-permute-start | bytes 25165832 | tf_op jit(solution)/shard_map/ppermute | solution.py:16
  778.8 8.6 copy-start.1
  778.8 8.6 copy-start.3
where the time goes:
time: 1070 us
  waiting for transfers between devices  466 us (44%)
  blocking collectives  232 us (22%)
  local copies, waits for them, and re-layouts  177 us (17%)
  matrix products  152 us (14%)
  starting transfers between devices  31.4 us (3%)
    all_to_all x1, waiting for transfers between devices, local(): lax.all_to_all(paired, 'slab', split_axis=1, concat_axis=0, tiled=True)  296 us
    all_to_all x1, blocking collectives, local(): lax.all_to_all(flattened, 'slab', split_axis=0, concat_axis=1, tiled=True)  232 us
    ppermute x2, waiting for transfers between devices, from_partner(): return lax.ppermute(block, axis, route)  171 us
    dot_general x6, matrix products, local(): jnp.einsum('rkb,kbc->rkc', crossing, weights[layer_index, 1], preferred_e...  81.4 us
    dot_general x6, matrix products, local(): jnp.einsum('rkb,kbc->rkc', current, weights[layer_index, 0], preferred_el...  70.2 us
    gather x6, local copies, waits for them, and re-layouts, local(): crossing = jnp.take(source, columns[layer_index], axis=1)  51.3 us
    another operation x2, local copies, waits for them, and re-layouts, local(): paired = jnp.stack([grouped, flipped], axis=2)  29.1 us
    ppermute x2, starting transfers between devices, from_partner(): return lax.ppermute(block, axis, route)  23.2 us
  transfers between devices with their start and end apart: 3, of which 3 were waited for; matrix products, arithmetic and copies ran while one was open for 2% of the time, Pallas kernels for 0%

commit v1 on v0

--- a/solution.py
+++ b/solution.py
@@ -4,6 +4,22 @@
 from jax.sharding import PartitionSpec as P
 
 ceiling = 4.0
+
+
+def swapped_with_each(array, axis, split, join):
+    ways, here = (lax.axis_size(axis), lax.axis_index(axis))
+    width = array.shape[split] // ways
+    shape = list(array.shape)
+    shape[split] = width
+    height = shape[join]
+    shape[join] = height * ways
+    full = jnp.zeros(shape, array.dtype)
+    for mask in range(ways):
+        part = lax.dynamic_slice_in_dim(array, (here ^ mask) * width, width, axis=split)
+        if mask:
+            part = lax.ppermute(part, axis, [(d, d ^ mask) for d in range(ways)])
+        full = lax.dynamic_update_slice_in_dim(full, part, (here ^ mask) * height, axis=join)
+    return full
 
 
 def from_partner(block, axis, bit):
@@ -35,7 +51,7 @@
     )
     flipped = flipped[:, :, ::-1].reshape(local_rows, slab_count, per_device * block_width)
     paired = jnp.stack([grouped, flipped], axis=2)
-    arrived = lax.all_to_all(paired, "slab", split_axis=1, concat_axis=0, tiled=True)
+    arrived = swapped_with_each(paired, "slab", 1, 0)
     current = arrived[:, 0, 0].reshape(-1, per_device, block_width)
     first_cross = arrived[:, 0, 1].reshape(-1, per_device, block_width)
     for layer_index in range(layer_count):

time: 1070 us -> 1260 us (1.18)
  local copies, waits for them, and re-layouts: 177 us -> 547 us
  waiting for transfers between devices: 466 us -> 319 us
  blocking collectives: 232 us -> 188 us
  starting transfers between devices: 31.4 us -> 15.3 us
  other arithmetic: 8.53 us -> 23.6 us
    dynamic_update_slice x0 -> x16, local copies, waits for them, and re-layouts: none -> 335 us  [swapped_with_each(): lax.dynamic_update_slice_in_dim(full, part, (here ^ mask) * height, axis=...]
    all_to_all x1 -> x0, waiting for transfers between devices: 296 us -> none  [local(): lax.all_to_all(paired, 'slab', split_axis=1, concat_axis=0, tiled=True)]
    ppermute x0 -> x15, waiting for transfers between devices: none -> 147 us  [swapped_with_each(): part = lax.ppermute(part, axis, [(d, d ^ mask) for d in range(ways)])]
    all_to_all x1, blocking collectives: 232 us -> 188 us  [local(): lax.all_to_all(flattened, 'slab', split_axis=0, concat_axis=1, tiled=True)]
    dynamic_slice x0 -> x15, local copies, waits for them, and re-layouts: none -> 38.1 us  [swapped_with_each(): lax.dynamic_slice_in_dim(array, (here ^ mask) * width, width, axis=split)]
    ppermute x0 -> x15, local copies, waits for them, and re-layouts: none -> 29.4 us  [swapped_with_each(): part = lax.ppermute(part, axis, [(d, d ^ mask) for d in range(ways)])]
    another operation x2 -> x0, local copies, waits for them, and re-layouts: 29.1 us -> none  [local(): paired = jnp.stack([grouped, flipped], axis=2)]
    ppermute x2, starting transfers between devices: 23.2 us -> 1.11 us  [from_partner(): return lax.ppermute(block, axis, route)]
  transfers between devices with their start and end apart: 3 -> 17, of which waited for: 3 -> 9; matrix products, arithmetic and copies ran while one was open for 2% -> 34% of each run, Pallas kernels for 0% -> 0%
where the time goes in v1:
time: 1260 us; the launch traced here: 1250 us
  local copies, waits for them, and re-layouts  547 us (43%)
  waiting for transfers between devices  319 us (25%)
  blocking collectives  188 us (15%)
  matrix products  152 us (12%)
  other arithmetic  23.6 us (2%)
  starting transfers between devices  15.3 us (1%)
    dynamic_update_slice x16, local copies, waits for them, and re-layouts, swapped_with_each(): lax.dynamic_update_slice_in_dim(full, part, (here ^ mask) * height, axis=...  335 us
    all_to_all x1, blocking collectives, local(): lax.all_to_all(flattened, 'slab', split_axis=0, concat_axis=1, tiled=True)  188 us
    ppermute x2, waiting for transfers between devices, from_partner(): return lax.ppermute(block, axis, route)  172 us
    ppermute x15, waiting for transfers between devices, swapped_with_each(): part = lax.ppermute(part, axis, [(d, d ^ mask) for d in range(ways)])  147 us
    dot_general x6, matrix products, local(): jnp.einsum('rkb,kbc->rkc', crossing, weights[layer_index, 1], preferred_e...  79.7 us
    dot_general x6, matrix products, local(): jnp.einsum('rkb,kbc->rkc', current, weights[layer_index, 0], preferred_el...  72.4 us
    gather x6, local copies, waits for them, and re-layouts, local(): crossing = jnp.take(source, columns[layer_index], axis=1)  51.5 us
    dynamic_slice x15, local copies, waits for them, and re-layouts, swapped_with_each(): lax.dynamic_slice_in_dim(array, (here ^ mask) * width, width, axis=split)  38.1 us
  transfers between devices with their start and end apart: 17, of which 9 were waited for; matrix products, arithmetic and copies ran while one was open for 34% of the time, Pallas kernels for 0%

profile of v1, /device:TPU:1, one launch (start us, length us, event | category | flops | bytes accessed | tf_op | source)
XLA Modules:
  0.0 1245.2 jit_solution(18279217723718533603)
XLA Ops:
  0.0 15.6 %copy.16 = bf16[64,65536]{0,1:T(8,128)(2,1)} copy(bf16[64,65536]{1,0:T(8,128)(2,1)} %param.6) | data formatting | bytes 16777216 | tf_op args[0]
  102.9 45.3 %collective-permute-done.1 = bf16[64,1,2,4096]{3,0,2,1:T(8,128)(2,1)} collective-permute-done((bf16[64,1,2,4096]{3,0,2,1:T(8,128)(2,1)}, bf16[64,1,2,4096]{3,0,2,1:T(8,128)(2,1)}, u32[]{:S(2)}, u32[]{:S(2)}) %collective-permute-start.1) | collective-permute-done | bytes 1048608 | tf_op jit(solution)/shard_map/ppermute | solution.py:20
  163.7 17.9 %collective-permute-done.7 = bf16[64,1,2,4096]{3,0,2,1:T(8,128)(2,1)} collective-permute-done((bf16[64,1,2,4096]{3,0,2,1:T(8,128)(2,1)}, bf16[64,1,2,4096]{3,0,2,1:T(8,128)(2,1)}, u32[]{:S(2)}, u32[]{:S(2)}) %collective-permute-start.7) | collective-permute-done | bytes 1048608 | tf_op jit(solution)/shard_map/ppermute | solution.py:20
  182.3 23.0 %collective-permute-done.5 = bf16[64,1,2,4096]{3,0,2,1:T(8,128)(2,1)} collective-permute-done((bf16[64,1,2,4096]{3,0,2,1:T(8,128)(2,1)}, bf16[64,1,2,4096]{3,0,2,1:T(8,128)(2,1)}, u32[]{:S(2)}, u32[]{:S(2)}) %collective-permute-start.5) | collective-permute-done | bytes 1048608 | tf_op jit(solution)/shard_map/ppermute | solution.py:20
  205.8 44.3 %collective-permute-done.4 = bf16[64,1,2,4096]{3,0,2,1:T(8,128)(2,1)} collective-permute-done((bf16[64,1,2,4096]{3,0,2,1:T(8,128)(2,1)}, bf16[64,1,2,4096]{3,0,2,1:T(8,128)(2,1)}, u32[]{:S(2)}, u32[]{:S(2)}) %collective-permute-start.4) | collective-permute-done | bytes 1048608 | tf_op jit(solution)/shard_map/ppermute | solution.py:20
  258.0 22.5 %dynamic_update_slice.48 = bf16[1024,1,2,4096]{0,3,2,1:T(8,128)(2,1)} dynamic-update-slice(bf16[1024,1,2,4096]{0,3,2,1:T(8,128)(2,1)} %broadcast_in_dim.12, bf16[64,1,2,4096]{0,3,2,1:T(8,128)(2,1)S(1)} %copy-done, s32[]{:T(128)S(6)} %select_n.104, s32[]{:T(128)} %constant.3.clone.1, s32[]{:T(128)} %constant.3.clone.1, s32[]{:T(128)} %constant.3.clone.1) | dynamic-update-slice | bytes 2097156 | tf_op jit(solution)/shard_map/dynamic_update_slice | solution.py:21
  283.2 19.8 %dynamic_update_slice.49 = bf16[1024,1,2,4096]{0,3,2,1:T(8,128)(2,1)} dynamic-update-slice(bf16[1024,1,2,4096]{0,3,2,1:T(8,128)(2,1)} %dynamic_update_slice.48, bf16[64,1,2,4096]{0,3,2,1:T(8,128)(2,1)S(1)} %copy.19, s32[]{:T(128)S(6)} %select_n.106, s32[]{:T(128)} %constant.3.clone.1, s32[]{:T(128)} %constant.3.clone.1, s32[]{:T(128)} %constant.3.clone.1) | dynamic-update-slice | bytes 2097156 | tf_op jit(solution)/shard_map/dynamic_update_slice | solution.py:21
  305.0 22.5 %dynamic_update_slice.50 = bf16[1024,1,2,4096]{0,3,2,1:T(8,128)(2,1)} dynamic-update-slice(bf16[1024,1,2,4096]{0,3,2,1:T(8,128)(2,1)} %dynamic_update_slice.49, bf16[64,1,2,4096]{0,3,2,1:T(8,128)(2,1)S(1)} %copy.21, s32[]{:T(128)S(6)} %select_n.108, s32[]{:T(128)} %constant.3.clone.1, s32[]{:T(128)} %constant.3.clone.1, s32[]{:T(128)} %constant.3.clone.1) | dynamic-update-slice | bytes 2097156 | tf_op jit(solution)/shard_map/dynamic_update_slice | solution.py:21
  329.5 19.5 %dynamic_update_slice.51 = bf16[1024,1,2,4096]{0,3,2,1:T(8,128)(2,1)} dynamic-update-slice(bf16[1024,1,2,4096]{0,3,2,1:T(8,128)(2,1)} %dynamic_update_slice.50, bf16[64,1,2,4096]{0,3,2,1:T(8,128)(2,1)S(1)} %copy.23, s32[]{:T(128)S(6)} %select_n.110, s32[]{:T(128)} %constant.3.clone.1, s32[]{:T(128)} %constant.3.clone.1, s32[]{:T(128)} %constant.3.clone.1) | dynamic-update-slice | bytes 2097156 | tf_op jit(solution)/shard_map/dynamic_update_slice | solution.py:21
  351.1 22.5 %dynamic_update_slice.52 = bf16[1024,1,2,4096]{0,3,2,1:T(8,128)(2,1)} dynamic-update-slice(bf16[1024,1,2,4096]{0,3,2,1:T(8,128)(2,1)} %dynamic_update_slice.51, bf16[64,1,2,4096]{0,3,2,1:T(8,128)(2,1)S(1)} %copy.25, s32[]{:T(128)S(6)} %select_n.112, s32[]{:T(128)} %constant.3.clone.1, s32[]{:T(128)} %constant.3.clone.1, s32[]{:T(128)} %constant.3.clone.1) | dynamic-update-slice | bytes 2097156 | tf_op jit(solution)/shard_map/dynamic_update_slice | solution.py:21
  375.6 19.5 %dynamic_update_slice.53 = bf16[1024,1,2,4096]{0,3,2,1:T(8,128)(2,1)} dynamic-update-slice(bf16[1024,1,2,4096]{0,3,2,1:T(8,128)(2,1)} %dynamic_update_slice.52, bf16[64,1,2,4096]{0,3,2,1:T(8,128)(2,1)S(1)} %copy.27, s32[]{:T(128)S(6)} %select_n.114, s32[]{:T(128)} %constant.3.clone.1, s32[]{:T(128)} %constant.3.clone.1, s32[]{:T(128)} %constant.3.clone.1) | dynamic-update-slice | bytes 2097156 | tf_op jit(solution)/shard_map/dynamic_update_slice | solution.py:21
  397.2 22.5 %dynamic_update_slice.54 = bf16[1024,1,2,4096]{0,3,2,1:T(8,128)(2,1)} dynamic-update-slice(bf16[1024,1,2,4096]{0,3,2,1:T(8,128)(2,1)} %dynamic_update_slice.53, bf16[64,1,2,4096]{0,3,2,1:T(8,128)(2,1)S(1)} %copy.29, s32[]{:T(128)S(6)} %select_n.116, s32[]{:T(128)} %constant.3.clone.1, s32[]{:T(128)} %constant.3.clone.1, s32[]{:T(128)} %constant.3.clone.1) | dynamic-update-slice | bytes 2097156 | tf_op jit(solution)/shard_map/dynamic_update_slice | solution.py:21
  421.7 19.6 %dynamic_update_slice.55 = bf16[1024,1,2,4096]{0,3,2,1:T(8,128)(2,1)} dynamic-update-slice(bf16[1024,1,2,4096]{0,3,2,1:T(8,128)(2,1)} %dynamic_update_slice.54, bf16[64,1,2,4096]{0,3,2,1:T(8,128)(2,1)S(1)} %copy.31, s32[]{:T(128)S(6)} %select_n.118, s32[]{:T(128)} %constant.3.clone.1, s32[]{:T(128)} %constant.3.clone.1, s32[]{:T(128)} %constant.3.clone.1) | dynamic-update-slice | bytes 2097156 | tf_op jit(solution)/shard_map/dynamic_update_slice | solution.py:21
  443.3 22.5 %dynamic_update_slice.56 = bf16[1024,1,2,4096]{0,3,2,1:T(8,128)(2,1)} dynamic-update-slice(bf16[1024,1,2,4096]{0,3,2,1:T(8,128)(2,1)} %dynamic_update_slice.55, bf16[64,1,2,4096]{0,3,2,1:T(8,128)(2,1)S(1)} %copy.33, s32[]{:T(128)S(6)} %select_n.120, s32[]{:T(128)} %constant.3.clone.1, s32[]{:T(128)} %constant.3.clone.1, s32[]{:T(128)} %constant.3.clone.1) | dynamic-update-slice | bytes 2097156 | tf_op jit(solution)/shard_map/dynamic_update_slice | solution.py:21
  467.9 19.6 %dynamic_update_slice.57 = bf16[1024,1,2,4096]{0,3,2,1:T(8,128)(2,1)} dynamic-update-slice(bf16[1024,1,2,4096]{0,3,2,1:T(8,128)(2,1)} %dynamic_update_slice.56, bf16[64,1,2,4096]{0,3,2,1:T(8,128)(2,1)S(1)} %copy.35, s32[]{:T(128)S(6)} %select_n.122, s32[]{:T(128)} %constant.3.clone.1, s32[]{:T(128)} %constant.3.clone.1, s32[]{:T(128)} %constant.3.clone.1) | dynamic-update-slice | bytes 2097156 | tf_op jit(solution)/shard_map/dynamic_update_slice | solution.py:21
  488.5 22.6 %dynamic_update_slice.58 = bf16[1024,1,2,4096]{0,3,2,1:T(8,128)(2,1)} dynamic-update-slice(bf16[1024,1,2,4096]{0,3,2,1:T(8,128)(2,1)} %dynamic_update_slice.57, bf16[64,1,2,4096]{0,3,2,1:T(8,128)(2,1)S(1)} %copy.37, s32[]{:T(128)S(6)} %select_n.124, s32[]{:T(128)} %constant.3.clone.1, s32[]{:T(128)} %constant.3.clone.1, s32[]{:T(128)} %constant.3.clone.1) | dynamic-update-slice | bytes 2097156 | tf_op jit(solution)/shard_map/dynamic_update_slice | solution.py:21
  513.1 19.6 %dynamic_update_slice.59 = bf16[1024,1,2,4096]{0,3,2,1:T(8,128)(2,1)} dynamic-update-slice(bf16[1024,1,2,4096]{0,3,2,1:T(8,128)(2,1)} %dynamic_update_slice.58, bf16[64,1,2,4096]{0,3,2,1:T(8,128)(2,1)S(1)} %copy.39, s32[]{:T(128)S(6)} %select_n.126, s32[]{:T(128)} %constant.3.clone.1, s32[]{:T(128)} %constant.3.clone.1, s32[]{:T(128)} %constant.3.clone.1) | dynamic-update-slice | bytes 2097156 | tf_op jit(solution)/shard_map/dynamic_update_slice | solution.py:21
  534.7 22.5 %dynamic_update_slice.60 = bf16[1024,1,2,4096]{0,3,2,1:T(8,128)(2,1)} dynamic-update-slice(bf16[1024,1,2,4096]{0,3,2,1:T(8,128)(2,1)} %dynamic_update_slice.59, bf16[64,1,2,4096]{0,3,2,1:T(8,128)(2,1)S(1)} %copy.41, s32[]{:T(128)S(6)} %select_n.128, s32[]{:T(128)} %constant.3.clone.1, s32[]{:T(128)} %constant.3.clone.1, s32[]{:T(128)} %constant.3.clone.1) | dynamic-update-slice | bytes 2097156 | tf_op jit(solution)/shard_map/dynamic_update_slice | solution.py:21
  559.3 19.6 %dynamic_update_slice.61 = bf16[1024,1,2,4096]{0,3,2,1:T(8,128)(2,1)} dynamic-update-slice(bf16[1024,1,2,4096]{0,3,2,1:T(8,128)(2,1)} %dynamic_update_slice.60, bf16[64,1,2,4096]{0,3,2,1:T(8,128)(2,1)S(1)} %copy.43, s32[]{:T(128)S(6)} %select_n.130, s32[]{:T(128)} %constant.3.clone.1, s32[]{:T(128)} %constant.3.clone.1, s32[]{:T(128)} %constant.3.clone.1) | dynamic-update-slice | bytes 2097156 | tf_op jit(solution)/shard_map/dynamic_update_slice | solution.py:21
  580.9 21.7 %dynamic_update_slice.62 = bf16[1024,1,2,4096]{0,3,2,1:T(8,128)(2,1)} dynamic-update-slice(bf16[1024,1,2,4096]{0,3,2,1:T(8,128)(2,1)} %dynamic_update_slice.61, bf16[64,1,2,4096]{0,3,2,1:T(8,128)(2,1)S(1)} %copy.45, s32[]{:T(128)S(6)} %select_n.132, s32[]{:T(128)} %constant.3.clone.1, s32[]{:T(128)} %constant.3.clone.1, s32[]{:T(128)} %constant.3.clone.1) | dynamic-update-slice | bytes 2097156 | tf_op jit(solution)/shard_map/dynamic_update_slice | solution.py:21
  604.6 18.7 %dynamic_update_slice.63 = bf16[1024,1,2,4096]{0,3,2,1:T(8,128)(2,1)} dynamic-update-slice(bf16[1024,1,2,4096]{0,3,2,1:T(8,128)(2,1)} %dynamic_update_slice.62, bf16[64,1,2,4096]{0,3,2,1:T(8,128)(2,1)S(1)} %copy.47, s32[]{:T(128)S(6)} %select_n.134, s32[]{:T(128)} %constant.3.clone.1, s32[]{:T(128)} %constant.3.clone.1, s32[]{:T(128)} %constant.3.clone.1) | dynamic-update-slice | bytes 2097156 | tf_op jit(solution)/shard_map/dynamic_update_slice | solution.py:21
  667.2 14.0 %fusion.34 = bf16[1024,32,128]{2,0,1:T(8,128)(2,1)} fusion(f32[32,128]{1,0:T(8,128)S(1)} %bitcast.129, f32[32,1024,128]{2,1,0:T(8,128)} %fusion.5, bf16[1024,32,128]{0,2,1:T(8,128)(2,1)} %bitcast.123, bf16[6,2,32,128,128]{4,3,2,1,0:T(8,128)(2,1)} %param.7), kind=kOutput, calls=%fused_computation.68 | convolution fusion | flops 1090519040 | bytes 34619392 | tf_op jit(solution)/shard_map/rkb,kbc->rkc/dot_general | solution.py:68
  726.9 170.5 %collective-permute-done.15 = bf16[1024,32,128]{2,0,1:T(8,128)(2,1)} collective-permute-done((bf16[1024,32,128]{2,0,1:T(8,128)(2,1)}, bf16[1024,32,128]{2,0,1:T(8,128)(2,1)}, u32[]{:S(2)}, u32[]{:S(2)}) %collective-permute-start.15) | collective-permute-done | bytes 8388640 | tf_op jit(solution)/shard_map/ppermute | solution.py:32
  1049.2 187.7 %all_to_all.19 = bf16[16,64,4096]{2,1,0:T(8,128)(2,1)} all-to-all(bf16[16,64,4096]{2,1,0:T(8,128)(2,1)} %all_to_all.14), channel_id=1, replica_groups=mesh['groups'=2,'slab'=16] {'slab'}, dimensions={0} | all-to-all | bytes 16777216 | tf_op jit(solution)/shard_map/all_to_all | solution.py:77
  (101 shorter events, 391.2 us)
Async XLA Ops:
  36.9 49.6 %collective-permute-start.9 = (bf16[64,1,2,4096]{3,0,2,1:T(8,128)(2,1)}, bf16[64,1,2,4096]{3,0,2,1:T(8,128)(2,1)S(1)}, u32[]{:S(2)}, u32[]{:S(2)}) collective-permute-start(bf16[64,1,2,4096]{3,0,2,1:T(8,128)(2,1)} %copy.36), channel_id=1, source_target_pairs={{0,10},{1,11},{2,8},{3,9},{4,14},{5,15},{6,12},{7,13},{8,2},{9,3},... | collective-permute-start | bytes 3145736 | tf_op jit(solution)/shard_map/ppermute | solution.py:20
  51.8 46.6 %collective-permute-start.3 = (bf16[64,1,2,4096]{3,0,2,1:T(8,128)(2,1)}, bf16[64,1,2,4096]{3,0,2,1:T(8,128)(2,1)}, u32[]{:S(2)}, u32[]{:S(2)}) collective-permute-start(bf16[64,1,2,4096]{3,0,2,1:T(8,128)(2,1)} %copy.24), channel_id=1, source_target_pairs={{0,4},{1,5},{2,6},{3,7},{4,0},{5,1},{6,2},{7,3},{8,12},{9,13},{10,... | collective-permute-start | bytes 3145736 | tf_op jit(solution)/shard_map/ppermute | solution.py:20
  55.9 46.9 %collective-permute-start.2 = (bf16[64,1,2,4096]{3,0,2,1:T(8,128)(2,1)}, bf16[64,1,2,4096]{3,0,2,1:T(8,128)(2,1)}, u32[]{:S(2)}, u32[]{:S(2)}) collective-permute-start(bf16[64,1,2,4096]{3,0,2,1:T(8,128)(2,1)} %copy.22), channel_id=1, source_target_pairs={{0,3},{1,2},{2,1},{3,0},{4,7},{5,6},{6,5},{7,4},{8,11},{9,10},{10,... | collective-permute-start | bytes 3145736 | tf_op jit(solution)/shard_map/ppermute | solution.py:20
  60.0 88.2 %collective-permute-start.1 = (bf16[64,1,2,4096]{3,0,2,1:T(8,128)(2,1)}, bf16[64,1,2,4096]{3,0,2,1:T(8,128)(2,1)}, u32[]{:S(2)}, u32[]{:S(2)}) collective-permute-start(bf16[64,1,2,4096]{3,0,2,1:T(8,128)(2,1)} %copy.20), channel_id=1, source_target_pairs={{0,2},{1,3},{2,0},{3,1},{4,6},{5,7},{6,4},{7,5},{8,10},{9,11},{10,... | collective-permute-start | bytes 3145736 | tf_op jit(solution)/shard_map/ppermute | solution.py:20
  63.7 84.5 %collective-permute-start = (bf16[64,1,2,4096]{3,0,2,1:T(8,128)(2,1)}, bf16[64,1,2,4096]{3,0,2,1:T(8,128)(2,1)}, u32[]{:S(2)}, u32[]{:S(2)}) collective-permute-start(bf16[64,1,2,4096]{3,0,2,1:T(8,128)(2,1)} %copy.18), channel_id=1, source_target_pairs={{0,1},{1,0},{2,3},{3,2},{4,5},{5,4},{6,7},{7,6},{8,9},{9,8},{10,11... | collective-permute-start | bytes 3145736 | tf_op jit(solution)/shard_map/ppermute | solution.py:20
  86.0 165.4 %copy-start.3 = (s32[6,32]{1,0:T(8,128)S(1)}, s32[6,32]{1,0:T(8,128)}, u32[]{:S(2)}) copy-start(s32[6,32]{1,0:T(8,128)} %param.9) | copy-start | bytes 2308
  86.5 76.4 %collective-permute-start.8 = (bf16[64,1,2,4096]{3,0,2,1:T(8,128)(2,1)}, bf16[64,1,2,4096]{3,0,2,1:T(8,128)(2,1)}, u32[]{:S(2)}, u32[]{:S(2)}) collective-permute-start(bf16[64,1,2,4096]{3,0,2,1:T(8,128)(2,1)} %copy.34), channel_id=1, source_target_pairs={{0,9},{1,8},{2,11},{3,10},{4,13},{5,12},{6,15},{7,14},{8,1},{9,0},... | collective-permute-start | bytes 3145736 | tf_op jit(solution)/shard_map/ppermute | solution.py:20
  98.5 83.1 %collective-permute-start.7 = (bf16[64,1,2,4096]{3,0,2,1:T(8,128)(2,1)}, bf16[64,1,2,4096]{3,0,2,1:T(8,128)(2,1)}, u32[]{:S(2)}, u32[]{:S(2)}) collective-permute-start(bf16[64,1,2,4096]{3,0,2,1:T(8,128)(2,1)} %copy.32), channel_id=1, source_target_pairs={{0,8},{1,9},{2,10},{3,11},{4,12},{5,13},{6,14},{7,15},{8,0},{9,1},... | collective-permute-start | bytes 3145736 | tf_op jit(solution)/shard_map/ppermute | solution.py:20
  102.9 78.7 %collective-permute-start.6 = (bf16[64,1,2,4096]{3,0,2,1:T(8,128)(2,1)}, bf16[64,1,2,4096]{3,0,2,1:T(8,128)(2,1)}, u32[]{:S(2)}, u32[]{:S(2)}) collective-permute-start(bf16[64,1,2,4096]{3,0,2,1:T(8,128)(2,1)} %copy.30), channel_id=1, source_target_pairs={{0,7},{1,6},{2,5},{3,4},{4,3},{5,2},{6,1},{7,0},{8,15},{9,14},{10,... | collective-permute-start | bytes 3145736 | tf_op jit(solution)/shard_map/ppermute | solution.py:20
  148.2 57.1 %collective-permute-start.5 = (bf16[64,1,2,4096]{3,0,2,1:T(8,128)(2,1)}, bf16[64,1,2,4096]{3,0,2,1:T(8,128)(2,1)}, u32[]{:S(2)}, u32[]{:S(2)}) collective-permute-start(bf16[64,1,2,4096]{3,0,2,1:T(8,128)(2,1)} %copy.28), channel_id=1, source_target_pairs={{0,6},{1,7},{2,4},{3,5},{4,2},{5,3},{6,0},{7,1},{8,14},{9,15},{10,... | collective-permute-start | bytes 3145736 | tf_op jit(solution)/shard_map/ppermute | solution.py:20
  148.2 101.9 %collective-permute-start.4 = (bf16[64,1,2,4096]{3,0,2,1:T(8,128)(2,1)}, bf16[64,1,2,4096]{3,0,2,1:T(8,128)(2,1)}, u32[]{:S(2)}, u32[]{:S(2)}) collective-permute-start(bf16[64,1,2,4096]{3,0,2,1:T(8,128)(2,1)} %copy.26), channel_id=1, source_target_pairs={{0,5},{1,4},{2,7},{3,6},{4,1},{5,0},{6,3},{7,2},{8,13},{9,12},{10,... | collective-permute-start | bytes 3145736 | tf_op jit(solution)/shard_map/ppermute | solution.py:20
  163.0 369.8 %collective-permute-start.11 = (bf16[64,1,2,4096]{3,0,2,1:T(8,128)(2,1)}, bf16[64,1,2,4096]{3,0,2,1:T(8,128)(2,1)}, u32[]{:S(2)}, u32[]{:S(2)}) collective-permute-start(bf16[64,1,2,4096]{3,0,2,1:T(8,128)(2,1)} %copy.40), channel_id=1, source_target_pairs={{0,12},{1,13},{2,14},{3,15},{4,8},{5,9},{6,10},{7,11},{8,4},{9,5},... | collective-permute-start | bytes 3145736 | tf_op jit(solution)/shard_map/ppermute | solution.py:20
  181.6 329.4 %collective-permute-start.10 = (bf16[64,1,2,4096]{3,0,2,1:T(8,128)(2,1)}, bf16[64,1,2,4096]{3,0,2,1:T(8,128)(2,1)}, u32[]{:S(2)}, u32[]{:S(2)}) collective-permute-start(bf16[64,1,2,4096]{3,0,2,1:T(8,128)(2,1)} %copy.38), channel_id=1, source_target_pairs={{0,11},{1,10},{2,9},{3,8},{4,15},{5,14},{6,13},{7,12},{8,3},{9,2},... | collective-permute-start | bytes 3145736 | tf_op jit(solution)/shard_map/ppermute | solution.py:20
  181.6 375.7 %collective-permute-start.12 = (bf16[64,1,2,4096]{3,0,2,1:T(8,128)(2,1)}, bf16[64,1,2,4096]{3,0,2,1:T(8,128)(2,1)}, u32[]{:S(2)}, u32[]{:S(2)}) collective-permute-start(bf16[64,1,2,4096]{3,0,2,1:T(8,128)(2,1)} %copy.42), channel_id=1, source_target_pairs={{0,13},{1,12},{2,15},{3,14},{4,9},{5,8},{6,11},{7,10},{8,5},{9,4},... | collective-permute-start | bytes 3145736 | tf_op jit(solution)/shard_map/ppermute | solution.py:20
  205.3 373.6 %collective-permute-start.13 = (bf16[64,1,2,4096]{3,0,2,1:T(8,128)(2,1)}, bf16[64,1,2,4096]{3,0,2,1:T(8,128)(2,1)}, u32[]{:S(2)}, u32[]{:S(2)}) collective-permute-start(bf16[64,1,2,4096]{3,0,2,1:T(8,128)(2,1)} %copy.44), channel_id=1, source_target_pairs={{0,14},{1,15},{2,12},{3,13},{4,10},{5,11},{6,8},{7,9},{8,6},{9,7},... | collective-permute-start | bytes 3145736 | tf_op jit(solution)/shard_map/ppermute | solution.py:20
  250.1 352.4 %collective-permute-start.14 = (bf16[64,1,2,4096]{3,0,2,1:T(8,128)(2,1)}, bf16[64,1,2,4096]{3,0,2,1:T(8,128)(2,1)}, u32[]{:S(2)}, u32[]{:S(2)}) collective-permute-start(bf16[64,1,2,4096]{3,0,2,1:T(8,128)(2,1)} %copy.46), channel_id=1, source_target_pairs={{0,15},{1,14},{2,13},{3,12},{4,11},{5,10},{6,9},{7,8},{8,7},{9,6},... | collective-permute-start | bytes 3145736 | tf_op jit(solution)/shard_map/ppermute | solution.py:20
  252.0 6.0 copy-start
  252.0 28.5 %copy-start.1 = (f32[6,4096]{1,0:T(8,128)S(1)}, f32[6,4096]{1,0:T(8,128)}, u32[]{:S(2)}) copy-start(f32[6,4096]{1,0:T(8,128)} %param.8) | copy-start | bytes 294916
  715.2 182.2 %collective-permute-start.15 = (bf16[1024,32,128]{2,0,1:T(8,128)(2,1)}, bf16[1024,32,128]{2,0,1:T(8,128)(2,1)}, u32[]{:S(2)}, u32[]{:S(2)}) collective-permute-start(bf16[1024,32,128]{2,0,1:T(8,128)(2,1)} %fusion.19), channel_id=1, source_target_pairs={{0,2},{2,0},{1,3},{3,1},{4,6},{6,4},{5,7},{7,5},{8,10},{10,8},{9,1... | collective-permute-start | bytes 25165832 | tf_op jit(solution)/shard_map/ppermute | solution.py:32
  953.2 14.2 %collective-permute-start.16 = (bf16[1024,32,128]{2,0,1:T(8,128)(2,1)}, bf16[1024,32,128]{2,0,1:T(8,128)(2,1)}, u32[]{:S(2)}, u32[]{:S(2)}) collective-permute-start(bf16[1024,32,128]{2,0,1:T(8,128)(2,1)} %fusion.25), channel_id=1, source_target_pairs={{0,1},{1,0},{2,3},{3,2},{4,5},{5,4},{6,7},{7,6},{8,9},{9,8},{10,11... | collective-permute-start | bytes 25165832 | tf_op jit(solution)/shard_map/ppermute | solution.py:32
  1001.3 8.6 copy-start.2
  1001.3 8.6 copy-start.4
